TPU v7x, 256 devices: a whole 4x4x8 slice. The times are simulated.
256 devices in a mesh: seq: 64 (over y, z, core), section: 4 (over x).
Axes of the slice: x: 4, y: 4, z: 8, core: 2. Of those that a mesh axis runs over, the one named last changes fastest.
Arguments:
- acts: bfloat16 [16384, 1408], P('seq'), may hold values from -16 to 16
- pre_act: bfloat16 [16384, 1536], P('seq', 'section'), may hold values from -6 to 6
- emb_grad: bfloat16 [8192, 1536], P('seq', 'section'), may hold values from -6 to 6
- filters: bfloat16 [7040, 1536], P('seq', 'section'), may hold values from -0.0625 to 0.0625
Outputs:
- input_grad: bfloat16 [16384, 1408], P('seq', 'section')
- filter_grad: float32 [7040, 1536], P('seq', 'section')
All inputs are finite; a program needn't handle non-finite values.
Results may differ from a plain program's by a relative error of at most 0.0049.
Values may be sent and summed in bfloat16 or wider, within the bound.
A program may use at most 128 MiB of HBM per device.

v0:
```python
import math
import jax
import jax.numpy as jnp
from jax import lax
from jax.sharding import PartitionSpec as P

KERNEL = 5
SEQS = 1


def with_halo(shard, sides, width):
    for axis, dim in sides:
        size, length = (lax.axis_size(axis), shard.shape[dim])
        up = [(i, (i + 1) % size) for i in range(size - 1)]
        down = [(j, i) for i, j in up]
        last = lax.slice_in_dim(shard, length - width, length, axis=dim)
        first = lax.slice_in_dim(shard, 0, width, axis=dim)
        before = lax.ppermute(last, axis, up)
        after = lax.ppermute(first, axis, down)
        shard = jnp.concatenate([before, shard, after], axis=dim)
    return shard


def gelu_slope(value):
    cumul = 0.5 * (1.0 + lax.erf(value * 0.7071067811865476))
    dens = jnp.exp(-0.5 * value * value) * 0.3989422804014327
    return cumul + value * dens


def shards(acts, pre_act, emb_grad, filters):
    rows = acts.shape[0]
    c_in = acts.shape[1]
    upward = jnp.repeat(emb_grad.astype(jnp.float32), 2, axis=0) * 0.5
    zvalue = pre_act.astype(jnp.float32)
    dz_grad = (upward * gelu_slope(zvalue)).astype(jnp.bfloat16)
    total_rows = rows * lax.axis_size("seq")
    length = total_rows // SEQS
    first = lax.axis_index("seq") * rows
    positions = first - 2 + jnp.arange(rows + 4, dtype=jnp.int32)
    inside = (jnp.floor_divide(positions, length) == first // length).astype(jnp.bfloat16)[:, None]
    scale_value = 1.0 / math.sqrt(total_rows)
    grad_rim = with_halo(dz_grad, (("seq", 0),), 2) * inside
    whole_term = (
        jnp.concatenate(
            [
                jnp.einsum(
                    "rc,ro->co",
                    acts,
                    grad_rim[4 - k : 4 - k + rows],
                    preferred_element_type=jnp.float32,
                )
                for k in range(KERNEL)
            ],
            axis=0,
        )
        * scale_value
    )
    piece = lax.all_gather(filters, "seq", axis=0, tiled=True)
    width = piece.shape[0]
    product = jnp.einsum("ro,no->rn", grad_rim, piece, preferred_element_type=jnp.float32)
    tap_of = jnp.arange(width, dtype=jnp.int32) // c_in
    total = jnp.zeros((rows, width), jnp.float32)
    for k in range(KERNEL):
        total = total + jnp.where((tap_of == k)[None, :], product[4 - k : 4 - k + rows], 0.0)
    partial_input = total.reshape(rows, KERNEL, c_in).sum(axis=1)
    input_grad = lax.psum_scatter(partial_input, "section", scatter_dimension=1, tiled=True).astype(
        jnp.bfloat16
    )
    filter_grad = lax.psum_scatter(whole_term, "seq", scatter_dimension=0, tiled=True)
    return (input_grad, filter_grad)


def solution(mesh):
    in_specs = (P("seq", None), P("seq", "section"), P("seq", "section"), P("seq", "section"))
    out_specs = (P("seq", "section"), P("seq", "section"))
    return jax.shard_map(shards, mesh=mesh, in_specs=in_specs, out_specs=out_specs, check_vma=False)
```

profile of v0, /device:TPU:8, one launch (start us, length us, event | category | flops | bytes accessed | tf_op | source)
XLA Modules:
  0.0 342.2 jit_solution(12863627836406627910)
XLA Ops:
  7.2 0.0 copy-start
  7.2 0.0 all-gather.3.cloned.1.call-start
  7.2 0.7 all-gather.3.cloned.1.call-update
  7.9 0.0 all-reduce.3.cloned.1.call-start
  8.0 0.9 convert_multiply_fusion.4
  8.9 0.1 broadcast_in_dim.46
  9.0 0.3 mul.55
  9.3 1.1 fusion.16
  10.4 7.1 %collective-permute-start.1 = (bf16[2,384]{1,0:T(2,128)(2,1)S(1)}, bf16[2,384]{1,0:T(2,128)(2,1)S(1)}, u32[]{:S(2)}, u32[]{:S(2)}) collective-permute-start(bf16[2,384]{1,0:T(2,128)(2,1)S(1)} %get-tuple-element.9), channel_id=1, source_target_pairs={{4,0},{8,4},{12,8},{16,12},{20,16},{24,20},{28,24},{32,28},{36,32}... | collective-permute-start | bytes 4616 | tf_op jit(solution)/shard_map/ppermute | solution.py:19
  17.5 1.9 collective-permute-start
  19.5 0.0 collective-permute-done.1
  19.5 5.0 %collective-permute-done = bf16[2,384]{1,0:T(2,128)(2,1)S(1)} collective-permute-done((bf16[2,384]{1,0:T(2,128)(2,1)S(1)}, bf16[2,384]{1,0:T(2,128)(2,1)S(1)}, u32[]{:S(2)}, u32[]{:S(2)}) %collective-permute-start) | collective-permute-done | bytes 1568 | tf_op jit(solution)/shard_map/ppermute | solution.py:18
  24.5 0.1 maximum_multiply_fusion
  24.6 0.0 copy-done
  24.7 0.5 fusion.8
  25.2 0.5 fusion.7
  25.7 0.5 fusion.6
  26.2 0.5 fusion.5
  26.7 0.5 fusion.4
  27.2 4.6 %broadcast_multiply_fusion = f32[7040,384]{0,1:T(8,128)} fusion(f32[7040,384]{0,1:T(8,128)S(1)} %fusion.4), kind=kLoop, calls=%fused_computation.9 | loop fusion | flops 2703360 | bytes 21626880 | tf_op jit(solution)/shard_map/mul | solution.py:44
  31.8 0.0 all-reduce.3.cloned.1.call-update
  31.8 0.0 reduce-scatter.3.cloned.1.call-start
  32.0 60.9 %all-gather.3.cloned.1.call-done = bf16[64,110,384]{2,1,0:T(8,128)(2,1)} async-done(((bf16[1,110,384]{2,1,0:T(8,128)(2,1)}), bf16[64,110,384]{2,1,0:T(8,128)(2,1)}) %all-gather.3.cloned.1.call-update) | async-done | bytes 5406736 | tf_op jit(solution)/shard_map/all_gather | solution.py:58
  92.9 7.7 %reshape.59 = bf16[7040,384]{1,0:T(8,128)(2,1)} reshape(bf16[64,110,384]{2,1,0:T(8,128)(2,1)} %all-gather.3.cloned.1.call-done) | data formatting | bytes 10813440
  100.6 4.7 %fusion.30 = f32[260,7040]{1,0:T(8,128)S(1)} fusion(bf16[7040,384]{1,0:T(8,128)(2,1)} %reshape.59, bf16[2,384]{1,0:T(2,128)(2,1)S(1)} %collective-permute-done.1, bf16[256,384]{1,0:T(8,128)(2,1)S(1)} %fusion.16, bf16[2,384]{1,0:T(2,128)(2,1)S(1)} %collective-permute-done, bf16[260]{0:T(512)(128)(2,1)S(1)} %fusion.29), kind=kOutput, calls=%fused_computation.63 | convolution fusion | flops 1406545920 | bytes 12928520 | tf_op jit(solution)/shard_map/ro,no->rn/dot_general | solution.py:60
  105.3 6.0 %fusion = f32[256,7040]{1,0:T(8,128)} fusion(f32[260,7040]{1,0:T(8,128)S(1)} %fusion.30, pred[7040]{0:T(1024)(128)(4,1)S(1)} %get-tuple-element.10, pred[7040]{0:T(1024)(128)(4,1)S(1)} %get-tuple-element.11, pred[7040]{0:T(1024)(128)(4,1)S(1)} %get-tuple-element.12, pred[7040]{0:T(1024)(128)(4,1)S(1)} %broadcast_compare_fusion.4, ...), kind=kLoop, calls=%fused_computation.1 | loop fusion | flops 16220160 | bytes 43288960 | tf_op jit(solution)/shard_map/add | solution.py:64
  111.3 0.0 copy-start.1
  111.3 8.8 %copy.9 = f32[256,7040]{0,1:T(8,128)} copy(f32[256,7040]{1,0:T(8,128)} %fusion) | data formatting | bytes 14417920 | tf_op jit(solution)/shard_map/add | solution.py:64
  120.1 0.0 copy-start.2
  120.1 4.9 %reduce_sum.9 = f32[256,1408]{0,1:T(8,128)} reduce(f32[256,5,1408]{0,2,1:T(8,128)} %bitcast.31, f32[]{:T(128)} %constant.61.clone.1), dimensions={1}, to_apply=%region_0.1 | reduce | flops 1441792 | bytes 8650756 | tf_op jit(solution)/shard_map/reduce_sum | solution.py:65
  125.0 0.0 reduce-scatter.3.cloned.1.call-update
  125.1 0.0 copy-done.2
  125.1 0.6 dynamic-slice
  126.3 178.5 %all-reduce.3.cloned.1.call-done = f32[7040,384]{0,1:T(8,128)} async-done(((f32[7040,384]{0,1:T(8,128)}), f32[7040,384]{0,1:T(8,128)}) %all-reduce.3.cloned.1.call-update) | async-done | bytes 10813456
  304.9 1.1 constant_dynamic-slice_fusion
  306.0 0.8 copy.10
  306.8 27.2 %reduce-scatter.3.cloned.1.call-done = f32[256,352]{0,1:T(8,128)} async-done(((f32[256,1408]{0,1:T(8,128)}), f32[256,352]{0,1:T(8,128)}) %reduce-scatter.3.cloned.1.call-update) | async-done | bytes 360464 | tf_op jit(solution)/shard_map/reduce_scatter | solution.py:66
  334.0 1.7 convert_element_type.23
  335.7 0.0 copy-done.1
  (5 shorter events, 0.1 us)
Async XLA Ops:
  7.2 17.5 %copy-start = (bf16[256,1408]{1,0:T(8,128)(2,1)S(1)}, bf16[256,1408]{1,0:T(8,128)(2,1)}, u32[]{:S(2)}) copy-start(bf16[256,1408]{1,0:T(8,128)(2,1)} %param.4) | copy-start | bytes 2162692
  7.2 85.7 %all-gather.3.cloned.1.call-start = ((), (), s32[]{:S(2)}) async-start(), calls=%async_computation.2 | async-start | bytes 5591040 | tf_op jit(solution)/shard_map/all_gather | solution.py:58
  7.9 297.0 %all-reduce.3.cloned.1.call-start = ((), (), s32[]{:S(2)}) async-start(), calls=%async_computation.3 | async-start | bytes 21626880
  10.4 9.1 %collective-permute-start.1 = (bf16[2,384]{1,0:T(2,128)(2,1)S(1)}, bf16[2,384]{1,0:T(2,128)(2,1)S(1)}, u32[]{:S(2)}, u32[]{:S(2)}) collective-permute-start(bf16[2,384]{1,0:T(2,128)(2,1)S(1)} %get-tuple-element.9), channel_id=1, source_target_pairs={{4,0},{8,4},{12,8},{16,12},{20,16},{24,20},{28,24},{32,28},{36,32}... | collective-permute-start | bytes 4616 | tf_op jit(solution)/shard_map/ppermute | solution.py:19
  17.5 7.0 %collective-permute-start = (bf16[2,384]{1,0:T(2,128)(2,1)S(1)}, bf16[2,384]{1,0:T(2,128)(2,1)S(1)}, u32[]{:S(2)}, u32[]{:S(2)}) collective-permute-start(bf16[2,384]{1,0:T(2,128)(2,1)S(1)} %get-tuple-element.8), channel_id=1, source_target_pairs={{0,4},{4,8},{8,12},{12,16},{16,20},{20,24},{24,28},{28,32},{32,36}... | collective-permute-start | bytes 4616 | tf_op jit(solution)/shard_map/ppermute | solution.py:18
  31.8 302.2 %reduce-scatter.3.cloned.1.call-start = ((), (), s32[]{:S(2)}) async-start(), calls=%async_computation.1 | async-start | bytes 1802240 | tf_op jit(solution)/shard_map/reduce_scatter | solution.py:66
  111.3 224.4 %copy-start.1 = (bf16[256,1408]{1,0:T(8,128)(2,1)S(1)}, bf16[256,1408]{1,0:T(8,128)(2,1)}, u32[]{:S(2)}) copy-start(bf16[256,1408]{1,0:T(8,128)(2,1)} %param.4) | copy-start | bytes 2162692
  120.1 5.0 %copy-start.2 = (u32[256]{0:T(256)S(1)}, u32[256]{0:T(256)}, u32[]{:S(2)}) copy-start(u32[256]{0:T(256)} %constant.69) | copy-start | bytes 3076
Sparse Core Ops, SparseCore 0:
  10.7 82.1 all-gather.2
  96.5 208.2 all-reduce.2
  307.6 26.3 reduce-scatter.2
where the time goes:
time: 343 us; the launch traced here: 342 us
  waiting for transfers between devices  272 us (79%)
  local copies, waits for them, and re-layouts  19.5 us (6%)
  other arithmetic  19.4 us (6%)
  between operations  14.6 us (4%)
  starting transfers between devices  9.13 us (3%)
  matrix products  7.19 us (2%)
    unnamed x4, waiting for transfers between devices  179 us
    all_gather x1, waiting for transfers between devices, shards(): piece = lax.all_gather(filters, 'seq', axis=0, tiled=True)  60.9 us
    reduce_scatter x1, waiting for transfers between devices, shards(): lax.psum_scatter(partial_input, 'section', scatter_dimension=1, tiled=True)  27.2 us
    unnamed x10, local copies, waits for them, and re-layouts  10.3 us
    add x1, local copies, waits for them, and re-layouts, shards(): total + jnp.where((tap_of == k)[None, :], product[4 - k:4 - k + rows], 0.0)  8.77 us
    ppermute x1, starting transfers between devices, with_halo(): after = lax.ppermute(first, axis, down)  7.09 us
  transfers between devices with their start and end apart: 5, of which 4 were waited for; matrix products, arithmetic and copies ran while one was open for 13% of the time, Pallas kernels for 0%

commit v1 on v0

--- a/solution.py
+++ b/solution.py
@@ -6,6 +6,15 @@
 
 KERNEL = 5
 SEQS = 1
+
+
+def match_the_sectors(block_in):
+    nodes = jax.lax.axis_size("seq")
+    y_new = range(block_in.ndim)
+    everything = map(lambda tick: nodes if tick == 0 else 1, y_new)
+    piece_out = list(everything)
+    all_values = jnp.tile(block_in, piece_out)
+    return jax.lax.all_to_all(all_values, axis_name="seq", split_axis=0, concat_axis=0, tiled=True)
 
 
 def with_halo(shard, sides, width):
@@ -55,7 +64,7 @@
         )
         * scale_value
     )
-    piece = lax.all_gather(filters, "seq", axis=0, tiled=True)
+    piece = match_the_sectors(filters)
     width = piece.shape[0]
     product = jnp.einsum("ro,no->rn", grad_rim, piece, preferred_element_type=jnp.float32)
     tap_of = jnp.arange(width, dtype=jnp.int32) // c_in

time: 343 us -> 374 us (1.090)
  waiting for transfers between devices: 272 us -> 290 us
  starting transfers between devices: 9.13 us -> 18.7 us
  local copies, waits for them, and re-layouts: 19.5 us -> 23.4 us
    ppermute x1, waiting for transfers between devices: 0.01 us -> 109 us  [with_halo(): after = lax.ppermute(first, axis, down)]
    all_gather x1 -> x0, waiting for transfers between devices: 60.9 us -> none  [shards(): piece = lax.all_gather(filters, 'seq', axis=0, tiled=True)]
    reduce_scatter x1, waiting for transfers between devices: 27.2 us -> 0.01 us  [shards(): lax.psum_scatter(partial_input, 'section', scatter_dimension=1, tiled=True)]
    all_to_all x0 -> x1, starting transfers between devices: none -> 12.4 us  [match_the_sectors(): jax.lax.all_to_all(all_values, axis_name='seq', split_axis=0, concat_axis...]
    all_to_all x0 -> x1, local copies, waits for them, and re-layouts: none -> 7.77 us  [match_the_sectors(): jax.lax.all_to_all(all_values, axis_name='seq', split_axis=0, concat_axis...]
    unnamed x10 -> x13, local copies, waits for them, and re-layouts: 10.3 us -> 2.53 us
    another operation x0 -> x1, local copies, waits for them, and re-layouts: none -> 3.9 us  [match_the_sectors(): all_values = jnp.tile(block_in, piece_out)]
    unnamed x4 -> x3, waiting for transfers between devices: 179 us -> 179 us
  transfers between devices with their start and end apart: 5 -> 5, of which waited for: 4 -> 3; matrix products, arithmetic and copies ran while one was open for 13% -> 9% of each run, Pallas kernels for 0% -> 0%
where the time goes in v1:
time: 374 us; the launch traced here: 373 us
  waiting for transfers between devices  290 us (78%)
  local copies, waits for them, and re-layouts  23.4 us (6%)
  starting transfers between devices  18.7 us (5%)
  other arithmetic  17.6 us (5%)
  between operations  16.3 us (4%)
  matrix products  7.19 us (2%)
    unnamed x3, waiting for transfers between devices  179 us
    ppermute x1, waiting for transfers between devices, with_halo(): after = lax.ppermute(first, axis, down)  109 us
    all_to_all x1, starting transfers between devices, match_the_sectors(): jax.lax.all_to_all(all_values, axis_name='seq', split_axis=0, concat_axis...  12.4 us
    add x1, local copies, waits for them, and re-layouts, shards(): total + jnp.where((tap_of == k)[None, :], product[4 - k:4 - k + rows], 0.0)  8.76 us
    all_to_all x1, local copies, waits for them, and re-layouts, match_the_sectors(): jax.lax.all_to_all(all_values, axis_name='seq', split_axis=0, concat_axis...  7.77 us
  transfers between devices with their start and end apart: 5, of which 3 were waited for; matrix products, arithmetic and copies ran while one was open for 9% of the time, Pallas kernels for 0%

profile of v1, /device:TPU:8, one launch (start us, length us, event | category | flops | bytes accessed | tf_op | source)
XLA Modules:
  0.0 373.3 jit_solution(4896163097983277382)
XLA Ops:
  8.0 0.0 copy-start
  8.0 0.0 copy-start.3
  8.0 3.9 %tile.2 = bf16[64,110,384]{2,1,0:T(8,128)(2,1)} broadcast(bf16[110,384]{1,0:T(8,128)(2,1)} %param.7), dimensions={1,2} | broadcast | bytes 5491200 | tf_op jit(solution)/shard_map/tile | solution.py:16
  11.9 0.0 copy-start.2
  11.9 12.4 %all-to-all-start = ((bf16[64,110,384]{2,1,0:T(8,128)(2,1)}), bf16[64,110,384]{2,1,0:T(8,128)(2,1)}, u32[]{:S(2)}, u32[]{:S(2)}) async-start(bf16[64,110,384]{2,1,0:T(8,128)(2,1)} %tile.2), calls=%async_computation | async-start | bytes 11010048 | tf_op jit(solution)/shard_map/all_to_all | solution.py:17
  24.3 0.0 all-reduce.3.cloned.1.call-start
  24.4 0.0 copy-done.3
  24.4 0.1 broadcast_in_dim.46
  24.6 0.3 mul.55
  24.9 0.0 copy-done.2
  24.9 0.2 fusion.16
  25.1 4.3 %collective-permute-start.1 = (bf16[2,384]{1,0:T(2,128)(2,1)S(1)}, bf16[2,384]{1,0:T(2,128)(2,1)S(1)}, u32[]{:S(2)}, u32[]{:S(2)}) collective-permute-start(bf16[2,384]{1,0:T(2,128)(2,1)S(1)} %get-tuple-element.9), channel_id=1, source_target_pairs={{4,0},{8,4},{12,8},{16,12},{20,16},{24,20},{28,24},{32,28},{36,32}... | collective-permute-start | bytes 4616 | tf_op jit(solution)/shard_map/ppermute | solution.py:28
  29.4 1.9 collective-permute-start
  31.4 109.3 %collective-permute-done.1 = bf16[2,384]{1,0:T(2,128)(2,1)S(1)} collective-permute-done((bf16[2,384]{1,0:T(2,128)(2,1)S(1)}, bf16[2,384]{1,0:T(2,128)(2,1)S(1)}, u32[]{:S(2)}, u32[]{:S(2)}) %collective-permute-start.1) | collective-permute-done | bytes 1568 | tf_op jit(solution)/shard_map/ppermute | solution.py:28
  140.7 2.0 collective-permute-done
  142.7 0.1 maximum_multiply_fusion
  142.8 0.0 copy-done
  142.8 0.5 fusion.8
  143.3 0.5 fusion.7
  143.8 0.5 fusion.6
  144.3 0.5 fusion.5
  144.8 0.5 fusion.4
  145.3 4.6 %broadcast_multiply_fusion = f32[7040,384]{0,1:T(8,128)} fusion(f32[7040,384]{0,1:T(8,128)S(1)} %fusion.4), kind=kLoop, calls=%fused_computation.9 | loop fusion | flops 2703360 | bytes 21626880 | tf_op jit(solution)/shard_map/mul | solution.py:53
  149.9 0.0 all-reduce.3.cloned.1.call-update
  150.0 0.0 reduce-scatter.3.cloned.1.call-start
  150.1 0.0 all-to-all-done
  150.1 7.8 %all_to_all.7 = bf16[7040,384]{1,0:T(8,128)(2,1)} reshape(bf16[64,110,384]{2,1,0:T(8,128)(2,1)} %all-to-all-done) | data formatting | bytes 10813440 | tf_op jit(solution)/shard_map/all_to_all | solution.py:17
  157.9 4.7 %fusion.30 = f32[260,7040]{1,0:T(8,128)S(1)} fusion(bf16[7040,384]{1,0:T(8,128)(2,1)} %all_to_all.7, bf16[2,384]{1,0:T(2,128)(2,1)S(1)} %collective-permute-done.1, bf16[256,384]{1,0:T(8,128)(2,1)S(1)} %fusion.16, bf16[2,384]{1,0:T(2,128)(2,1)S(1)} %collective-permute-done, bf16[260]{0:T(512)(128)(2,1)S(1)} %fusion.29), kind=kOutput, calls=%fused_computation.63 | convolution fusion | flops 1406545920 | bytes 12928520 | tf_op jit(solution)/shard_map/ro,no->rn/dot_general | solution.py:69
  162.6 6.0 %fusion = f32[256,7040]{1,0:T(8,128)} fusion(f32[260,7040]{1,0:T(8,128)S(1)} %fusion.30, pred[7040]{0:T(1024)(128)(4,1)S(1)} %get-tuple-element.10, pred[7040]{0:T(1024)(128)(4,1)S(1)} %get-tuple-element.11, pred[7040]{0:T(1024)(128)(4,1)S(1)} %get-tuple-element.12, pred[7040]{0:T(1024)(128)(4,1)S(1)} %broadcast_compare_fusion.4, ...), kind=kLoop, calls=%fused_computation.1 | loop fusion | flops 16220160 | bytes 43288960 | tf_op jit(solution)/shard_map/add | solution.py:73
  168.6 0.0 copy-start.1
  168.6 8.8 %copy.9 = f32[256,7040]{0,1:T(8,128)} copy(f32[256,7040]{1,0:T(8,128)} %fusion) | data formatting | bytes 14417920 | tf_op jit(solution)/shard_map/add | solution.py:73
  177.3 0.0 copy-start.4
  177.3 4.9 %reduce_sum.9 = f32[256,1408]{0,1:T(8,128)} reduce(f32[256,5,1408]{0,2,1:T(8,128)} %bitcast.30, f32[]{:T(128)} %constant.61.clone.1), dimensions={1}, to_apply=%region_0.1 | reduce | flops 1441792 | bytes 8650756 | tf_op jit(solution)/shard_map/reduce_sum | solution.py:74
  182.3 0.0 reduce-scatter.3.cloned.1.call-update
  182.3 0.0 copy-done.4
  182.3 0.6 dynamic-slice
  183.5 178.7 %all-reduce.3.cloned.1.call-done = f32[7040,384]{0,1:T(8,128)} async-done(((f32[7040,384]{0,1:T(8,128)}), f32[7040,384]{0,1:T(8,128)}) %all-reduce.3.cloned.1.call-update) | async-done | bytes 10813456
  362.3 1.1 constant_dynamic-slice_fusion
  363.4 0.8 copy.10
  364.2 0.0 reduce-scatter.3.cloned.1.call-done
  364.2 1.7 convert_element_type.23
  365.9 0.0 copy-done.1
  (6 shorter events, 0.1 us)
Async XLA Ops:
  8.0 134.8 %copy-start = (bf16[256,1408]{1,0:T(8,128)(2,1)S(1)}, bf16[256,1408]{1,0:T(8,128)(2,1)}, u32[]{:S(2)}) copy-start(bf16[256,1408]{1,0:T(8,128)(2,1)} %param.4) | copy-start | bytes 2162692
  8.0 16.4 %copy-start.3 = (bf16[128,384]{1,0:T(8,128)(2,1)S(1)}, bf16[128,384]{1,0:T(8,128)(2,1)}, u32[]{:S(2)}) copy-start(bf16[128,384]{1,0:T(8,128)(2,1)} %param.6) | copy-start | bytes 294916
  11.9 12.9 %copy-start.2 = (bf16[256,384]{1,0:T(8,128)(2,1)S(1)}, bf16[256,384]{1,0:T(8,128)(2,1)}, u32[]{:S(2)}) copy-start(bf16[256,384]{1,0:T(8,128)(2,1)} %param.5) | copy-start | bytes 589828
  11.9 138.2 %all-to-all-start = ((bf16[64,110,384]{2,1,0:T(8,128)(2,1)}), bf16[64,110,384]{2,1,0:T(8,128)(2,1)}, u32[]{:S(2)}, u32[]{:S(2)}) async-start(bf16[64,110,384]{2,1,0:T(8,128)(2,1)} %tile.2), calls=%async_computation | async-start | bytes 11010048 | tf_op jit(solution)/shard_map/all_to_all | solution.py:17
  24.3 337.9 %all-reduce.3.cloned.1.call-start = ((), (), s32[]{:S(2)}) async-start(), calls=%async_computation.3 | async-start | bytes 21626880
  25.1 115.6 %collective-permute-start.1 = (bf16[2,384]{1,0:T(2,128)(2,1)S(1)}, bf16[2,384]{1,0:T(2,128)(2,1)S(1)}, u32[]{:S(2)}, u32[]{:S(2)}) collective-permute-start(bf16[2,384]{1,0:T(2,128)(2,1)S(1)} %get-tuple-element.9), channel_id=1, source_target_pairs={{4,0},{8,4},{12,8},{16,12},{20,16},{24,20},{28,24},{32,28},{36,32}... | collective-permute-start | bytes 4616 | tf_op jit(solution)/shard_map/ppermute | solution.py:28
  29.4 113.3 %collective-permute-start = (bf16[2,384]{1,0:T(2,128)(2,1)S(1)}, bf16[2,384]{1,0:T(2,128)(2,1)S(1)}, u32[]{:S(2)}, u32[]{:S(2)}) collective-permute-start(bf16[2,384]{1,0:T(2,128)(2,1)S(1)} %get-tuple-element.8), channel_id=1, source_target_pairs={{0,4},{4,8},{8,12},{12,16},{16,20},{20,24},{24,28},{28,32},{32,36}... | collective-permute-start | bytes 4616 | tf_op jit(solution)/shard_map/ppermute | solution.py:27
  150.0 214.3 %reduce-scatter.3.cloned.1.call-start = ((), (), s32[]{:S(2)}) async-start(), calls=%async_computation.2 | async-start | bytes 1802240 | tf_op jit(solution)/shard_map/reduce_scatter | solution.py:75
  168.6 197.3 %copy-start.1 = (bf16[256,1408]{1,0:T(8,128)(2,1)S(1)}, bf16[256,1408]{1,0:T(8,128)(2,1)}, u32[]{:S(2)}) copy-start(bf16[256,1408]{1,0:T(8,128)(2,1)} %param.4) | copy-start | bytes 2162692
  177.3 5.0 %copy-start.4 = (u32[256]{0:T(256)S(1)}, u32[256]{0:T(256)}, u32[]{:S(2)}) copy-start(u32[256]{0:T(256)} %constant.69) | copy-start | bytes 3076
Sparse Core Ops, SparseCore 0:
  150.1 212.1 all-reduce.2
Sparse Core Ops, SparseCore 1:
  182.4 29.2 reduce-scatter.2
